TPU v7x, 128 devices: a whole 4x4x4 slice. The times are simulated.
128 devices in a mesh: section: 2 (over x_hi), tp: 2 (over core), dp: 32 (over z, y, x_lo).
Axes of the slice: x: 4 (x_hi: 2, x_lo: 2; x = x_hi * 2 + x_lo), y: 4, z: 4, core: 2. Of those that a mesh axis runs over, the one named last changes fastest.
Arguments:
- tokens_in: bfloat16 [32, 512, 4096], P('dp', None, 'tp'), may hold values from -6 to 6
- patches: bfloat16 [32, 256, 32], P('dp'), may hold values from -6 to 6
- segment_ids: int32 [32, 512], P('dp'), may hold values from 0 to 3, never falling along the last dimension, each value on 1 to 256 neighbouring positions
- img_start: int32 [32], P('dp'), may hold values from 0 to 256
- img_count: int32 [32], P('dp'), may hold values from 0 to 1
- norm_gain: float32 [2, 4096], P('section'), may hold values from 0.1 to 1.9
- w_qkv: bfloat16 [2, 4096, 16, 3, 128], P('section', 'dp', 'tp'), may hold values from -2 to 2
- w_out: bfloat16 [2, 2048, 4096], P('section', 'dp', 'tp'), may hold values from -0.125 to 0.125
- w_down1: bfloat16 [32, 512], replicated, may hold values from -1 to 1
- w_down2: bfloat16 [512, 4096], P(None, 'tp'), may hold values from -0.25 to 0.25
- w_up1: bfloat16 [4096, 512], P('tp'), may hold values from -0.09375 to 0.09375
- w_up2: bfloat16 [512, 32], P(None, 'section'), may hold values from -0.25 to 0.25
- cotangent: bfloat16 [32, 256, 32], P('dp', None, 'section'), may hold values from -6 to 6
Outputs:
- hidden_states: bfloat16 [2, 32, 512, 4096], P('section', 'dp', None, 'tp')
- image_pred: bfloat16 [32, 256, 32], P('dp', None, 'section')
- grad_up: float32 [512, 32], P(None, 'section')
Inputs may be any that keep to these rules, and one draw needn't show every extreme that they name: `segment_ids`: document of each position; never falls along a micro-batch, each document covers 1 to 256 positions.
All inputs are finite; a program needn't handle non-finite values.
Results may differ from a plain program's by a relative error of at most 0.019.
Values may be sent and summed in bfloat16 or wider, within the bound.
A program may use at most 128 MiB of HBM per device.

v0:
```python
import math
import jax
import jax.numpy as jnp
from jax import lax
from jax.sharding import PartitionSpec as P

EPSILON = 1e-05


def passed_along(value, axis, by):
    count = lax.axis_size(axis)
    pairs = [(i, i + by) for i in range(count) if 0 <= i + by < count]
    return lax.ppermute(value, axis, pairs)


def broadcast(block, axis, holder):
    block = jnp.where(lax.axis_index(axis) == holder, block, jnp.zeros_like(block))
    return lax.psum(block, axis)


def unet_down(patches, w_down1, w_down2):
    inner = jnp.einsum("mkp,pc->mkc", patches, w_down1, preferred_element_type=jnp.float32)
    skipped = jax.nn.silu(inner).astype(jnp.bfloat16)
    tokens = jnp.einsum("mkc,cd->mkd", skipped, w_down2, preferred_element_type=jnp.float32)
    return (skipped, tokens.astype(jnp.bfloat16))


def place_images(tokens_in, image_tokens, img_start, img_count):

    def single(rows, image, start, count):
        placed = lax.dynamic_update_slice_in_dim(rows, image, start, 0)
        return jnp.where(count > 0, placed, rows)

    return jax.vmap(single)(tokens_in, image_tokens, img_start, img_count)


def allowed_pairs(segment, start, count, rows, img_tok):
    position = jnp.arange(rows, dtype=jnp.int32)
    in_image = (count > 0) & (position >= start) & (position < start + img_tok)
    same = segment[:, None] == segment[None, :]
    causal = position[None, :] <= position[:, None]
    return same & (causal | in_image[:, None] & in_image[None, :])


def rms_normed(full, gain):
    values = full.astype(jnp.float32)
    mean_sq = jnp.mean(values * values, axis=-1, keepdims=True)
    return (values * lax.rsqrt(mean_sq + EPSILON) * gain).astype(jnp.bfloat16)


def attend(normed, weights_qkv, allowed):
    heads, hdim = (weights_qkv.shape[1], weights_qkv.shape[3])
    proj = jnp.einsum(
        "rd,dhtk->htrk", normed, weights_qkv, preferred_element_type=jnp.float32
    ).astype(jnp.bfloat16)

    def one_head(triple):
        query, keys, values = (triple[0], triple[1], triple[2])
        scores = jnp.dot(query, keys.T, preferred_element_type=jnp.float32) / math.sqrt(hdim)
        scores = jnp.where(allowed, scores, -1e30)
        probs = jnp.exp(scores - jnp.max(scores, axis=-1, keepdims=True))
        probs = (probs / jnp.sum(probs, axis=-1, keepdims=True)).astype(jnp.bfloat16)
        return jnp.dot(probs, values, preferred_element_type=jnp.float32).astype(jnp.bfloat16)

    mixed = lax.map(one_head, proj)
    return jnp.transpose(mixed, (1, 0, 2)).reshape(mixed.shape[1], heads * hdim)


def shards(
    tokens_in,
    patches,
    segment_ids,
    img_start,
    img_count,
    norm_gain,
    w_qkv,
    w_out,
    w_down1,
    w_down2,
    w_up1,
    w_up2,
    cotangent,
):
    n_section = lax.axis_size("section")
    section = lax.axis_index("section")
    final = n_section - 1
    micro, rows, width = tokens_in.shape
    img_tok = patches.shape[1]
    channels = w_down1.shape[1]
    qkv_full, out_full = (
        lax.all_gather(w_qkv, "dp", axis=1, tiled=True),
        lax.all_gather(w_out, "dp", axis=1, tiled=True),
    )
    qkv_layer = qkv_full[0]
    out_layer = out_full[0]
    gain = norm_gain[0]
    needs_down = section == 0

    def run_down(unused):
        return unet_down(patches, w_down1, w_down2)

    def no_down(unused):
        return (
            jnp.zeros((micro, img_tok, channels), jnp.bfloat16),
            jnp.zeros((micro, img_tok, width), jnp.bfloat16),
        )

    skipped, image_tokens = lax.cond(needs_down, run_down, no_down, 0)
    embedded = place_images(tokens_in, image_tokens, img_start, img_count)
    masks = jax.vmap(lambda seg, st, ct: allowed_pairs(seg, st, ct, rows, img_tok))(
        segment_ids, img_start, img_count
    )
    local_width = qkv_layer.shape[1] * qkv_layer.shape[3]

    def tick(carry, step):
        inbox, skip_box, outputs, kept = carry
        index = step - section
        live = (index >= 0) & (index < micro)
        slot = jnp.clip(index, 0, micro - 1)
        current = jnp.where(section == 0, lax.dynamic_index_in_dim(embedded, slot, 0, False), inbox)
        allowed = lax.dynamic_index_in_dim(masks, slot, 0, False)
        full = lax.all_gather(current, "tp", axis=1, tiled=True)

        def attend_live(unused):
            return attend(rms_normed(full, gain), qkv_layer, allowed)

        def attend_spare(unused):
            return jnp.zeros((rows, local_width), jnp.bfloat16)

        local_heads = lax.cond(live, attend_live, attend_spare, 0)
        all_heads = lax.all_gather(local_heads, "tp", axis=1, tiled=True)

        def project_live(unused):
            added = jnp.dot(all_heads, out_layer, preferred_element_type=jnp.float32)
            return (current.astype(jnp.float32) + added).astype(jnp.bfloat16)

        def project_spare(unused):
            return current

        result = lax.cond(live, project_live, project_spare, 0)
        previous = lax.dynamic_index_in_dim(outputs, slot, 0, False)
        outputs = lax.dynamic_update_index_in_dim(
            outputs, jnp.where(live, result, previous), slot, 0
        )
        outgoing = jnp.where(
            section == 0, lax.dynamic_index_in_dim(skipped, slot, 0, False), skip_box
        )
        stored = lax.dynamic_index_in_dim(kept, slot, 0, False)
        kept = lax.dynamic_update_index_in_dim(
            kept, jnp.where(live & (section == final), skip_box, stored), slot, 0
        )
        inbox, skip_box = passed_along((result, outgoing), "section", 1)
        return ((inbox, skip_box, outputs, kept), None)

    start_carry = (
        jnp.zeros((rows, width), jnp.bfloat16),
        jnp.zeros((img_tok, channels), jnp.bfloat16),
        jnp.zeros((micro, rows, width), jnp.bfloat16),
        jnp.zeros((micro, img_tok, channels), jnp.bfloat16),
    )
    ticks = micro + n_section - 1
    carry, unused = lax.scan(tick, start_carry, jnp.arange(ticks, dtype=jnp.int32))
    outputs = carry[2]
    skip_store = carry[3]
    final_rows = jax.vmap(lambda block, st: lax.dynamic_slice_in_dim(block, st, img_tok, 0))(
        outputs, img_start
    )
    partial_value = jnp.einsum("mkd,dc->mkc", final_rows, w_up1, preferred_element_type=jnp.float32)
    summed = lax.psum(partial_value.astype(jnp.bfloat16), "tp").astype(jnp.float32)
    upper = jax.nn.silu(summed + skip_store.astype(jnp.float32)).astype(jnp.bfloat16)
    upper = broadcast(upper, "section", final)
    present = (img_count > 0)[:, None, None]
    projected = jnp.einsum("mkc,cp->mkp", upper, w_up2, preferred_element_type=jnp.float32)
    image_pred = jnp.where(present, projected, 0.0).astype(jnp.bfloat16)
    weighted = jnp.where(present, cotangent, jnp.zeros_like(cotangent))
    grad_local = jnp.einsum("mkc,mkp->cp", upper, weighted, preferred_element_type=jnp.float32)
    grad_up = lax.psum(grad_local.astype(jnp.bfloat16), "dp").astype(jnp.float32)
    return (outputs[None], image_pred, grad_up)


def solution(mesh):
    placed = (
        P("dp", None, "tp"),
        P("dp", None, None),
        P("dp", None),
        P("dp"),
        P("dp"),
        P("section", None),
        P("section", "dp", "tp", None, None),
        P("section", "dp", "tp"),
        P(),
        P(None, "tp"),
        P("tp", None),
        P(None, "section"),
        P("dp", None, "section"),
    )
    return jax.shard_map(
        shards,
        mesh=mesh,
        in_specs=placed,
        out_specs=(P("section", "dp", None, "tp"), P("dp", None, "section"), P(None, "section")),
        check_vma=False,
    )
```

profile of v0, /device:TPU:0, one launch (start us, length us, event | category | flops | bytes accessed | tf_op | source)
XLA Modules:
  0.0 1289.1 jit_solution(7725941785170714117)
XLA Ops:
  7.2 3.3 copy.63
  13.1 3.4 conditional.3
  17.4 1.9 and_reduce_fusion
  19.3 3.1 select_select_fusion
  22.4 6.4 select_n.85
  28.9 174.6 %all-gather.7.cloned.1.call-done = bf16[1,2048,2048]{2,1,0:T(8,128)(2,1)} async-done(((bf16[1,64,2048]{2,1,0:T(8,128)(2,1)}), bf16[1,2048,2048]{2,1,0:T(8,128)(2,1)}) %all-gather.7.cloned.1.call-update) | async-done | bytes 8388624 | tf_op jit(solution)/shard_map/all_gather | solution.py:92
  203.5 536.5 %all-gather.5.cloned.1.call-done = bf16[1,4096,8,3,128]{4,1,3,2,0:T(8,128)(2,1)} async-done(((bf16[1,128,8,3,128]{4,1,3,2,0:T(8,128)(2,1)}), bf16[1,4096,8,3,128]{4,1,3,2,0:T(8,128)(2,1)}) %all-gather.5.cloned.1.call-update) | async-done | bytes 25165840 | tf_op jit(solution)/shard_map/all_gather | solution.py:91
  744.6 311.7 %while.30 = (s32[]{:T(128)}, bf16[512,2048]{1,0:T(8,128)(2,1)}, bf16[256,512]{1,0:T(8,128)(2,1)}, bf16[1,512,2048]{2,1,0:T(8,128)(2,1)}, bf16[1,256,512]{2,1,0:T...) while((s32[]{:T(128)}, bf16[512,2048]{1,0:T(8,128)(2,1)}, ...), condition=%wide.region_13.14_spmd.clone, body=%wide.region_3.13_spmd.clone.sunk | while | flops 17339318272 | bytes 138717024 | solution.py:162
  744.6 3.2 bitcast_select_fusion.5
  749.2 14.0 %all-gather.9.cloned.1.call-done = bf16[512,4096]{1,0:T(8,128)(2,1)} async-done(((bf16[512,2048]{1,0:T(8,128)(2,1)}), bf16[512,4096]{1,0:T(8,128)(2,1)}) %all-gather.9.cloned.1.call-update) | async-done | bytes 4194320 | tf_op jit(solution)/shard_map/while/body/eval_jaxpr/all_gather | solution.py:122
  764.4 53.1 %conditional.8 = (bf16[512,1024]{1,0:T(8,128)(2,1)S(1)}) conditional(s32[]{:T(128)} %convert_element_type.134, () %tuple.85, (bf16[512,4096]{1,0:T(8,128)(2,1)}, f32[1,4096]{1,0:T(1,128)S(1)}, bf16[4096,8,3,128]{3,0,2,1:T(8,128)(2,1)}, s32[512]{0:T(512)S(1)}, s32[1,512,512]{1,2,0:T(8,128)S(1)}, /*index=5*/s32[512]{0:T(512)S(1)}, ...), branch_computations={%region_4.4_spmd, %region_5.10_spmd} | conditional | flops 13038844928 | bytes 61908192 | solution.py:130
  764.4 3.2 fusion.12
  767.8 19.1 %convert_bitcast_fusion = bf16[8,3,512,128]{3,2,1,0:T(8,128)(2,1)} fusion(bf16[4096,8,3,128]{3,0,2,1:T(8,128)(2,1)} %get-tuple-element.178, bf16[512,4096]{1,0:T(8,128)(2,1)S(1)} %copy-done.1, f32[4096]{0:T(1024)S(1)} %bitcast.118, f32[512]{0:T(512)S(1)} %add_rsqrt_fusion), kind=kOutput, calls=%fused_computation.29 | convolution fusion | flops 12894863360 | bytes 32524288 | tf_op jit(solution)/shard_map/while/body/eval_jaxpr/cond/branch_1_fun/rd,dhtk->htrk/dot_general | solution.py:53
  788.5 27.5 %while.29 = (s32[]{:T(128)}, bf16[8,512,128]{2,1,0:T(8,128)(2,1)}, bf16[8,3,512,128]{3,2,1,0:T(8,128)(2,1)}, pred[512,512]{0,1:T(32,128)(4,1)S(1)}, s32[]{:T(128)}, /*index=5*/s32[]{:T(128)}, s32[]{}, s32[]{}) while((s32[]{:T(128)}, bf16[8,512,128]{2,1,0:T(8,128)(2,1)}, bf16[8,3,512,128]{3,2,1,0:T(8,128)(2,1)}, ...), condition=%wide.region_10.9_spmd, body=%wide.region_7.8_spmd.sunk | while | flops 136379392 | bytes 3944565 | solution.py:65
  810.7 1.9 fusion.61
  814.1 1.9 fusion.61
  818.5 13.3 %all-gather.11.cloned.1.call-done = bf16[512,2048]{1,0:T(8,128)(2,1)} async-done(((bf16[512,1024]{1,0:T(8,128)(2,1)}), bf16[512,2048]{1,0:T(8,128)(2,1)}) %all-gather.11.cloned.1.call-update) | async-done | bytes 2097168 | tf_op jit(solution)/shard_map/while/body/eval_jaxpr/all_gather | solution.py:131
  831.7 10.5 conditional.9
  831.7 10.5 add_convert_fusion
  842.2 2.6 collective-permute-start
  847.2 3.8 fusion.58
  850.9 44.0 %collective-permute-done.1 = bf16[256,512]{1,0:T(8,128)(2,1)S(1)} collective-permute-done((bf16[256,512]{1,0:T(8,128)(2,1)S(1)}, bf16[256,512]{1,0:T(8,128)(2,1)S(1)}, u32[]{:S(2)}, u32[]{:S(2)}) %collective-permute-start.1) | collective-permute-done | bytes 262176 | tf_op jit(solution)/shard_map/while/body/eval_jaxpr/ppermute | solution.py:13
  895.6 3.1 bitcast_select_fusion.5
  900.2 18.7 %all-gather.9.cloned.1.call-done = bf16[512,4096]{1,0:T(8,128)(2,1)} async-done(((bf16[512,2048]{1,0:T(8,128)(2,1)}), bf16[512,4096]{1,0:T(8,128)(2,1)}) %all-gather.9.cloned.1.call-update) | async-done | bytes 4194320 | tf_op jit(solution)/shard_map/while/body/eval_jaxpr/all_gather | solution.py:122
  921.3 67.7 %all-gather.11.cloned.1.call-done = bf16[512,2048]{1,0:T(8,128)(2,1)} async-done(((bf16[512,1024]{1,0:T(8,128)(2,1)}), bf16[512,2048]{1,0:T(8,128)(2,1)}) %all-gather.11.cloned.1.call-update) | async-done | bytes 2097168 | tf_op jit(solution)/shard_map/while/body/eval_jaxpr/all_gather | solution.py:131
  989.0 16.7 %collective-permute-start = (bf16[512,2048]{1,0:T(8,128)(2,1)}, bf16[512,2048]{1,0:T(8,128)(2,1)}, u32[]{:S(2)}, u32[]{:S(2)}) collective-permute-start(bf16[512,2048]{1,0:T(8,128)(2,1)} %get-tuple-element.540), channel_id=1, source_target_pairs={{0,64},{1,65},{2,66},{3,67},{4,68},{5,69},{6,70},{7,71},{8,72},{9,... | collective-permute-start | bytes 6291464 | tf_op jit(solution)/shard_map/while/body/eval_jaxpr/ppermute | solution.py:13
  1008.1 3.1 fusion.58
  1011.3 44.3 %collective-permute-done.1 = bf16[256,512]{1,0:T(8,128)(2,1)S(1)} collective-permute-done((bf16[256,512]{1,0:T(8,128)(2,1)S(1)}, bf16[256,512]{1,0:T(8,128)(2,1)S(1)}, u32[]{:S(2)}, u32[]{:S(2)}) %collective-permute-start.1) | collective-permute-done | bytes 262176 | tf_op jit(solution)/shard_map/while/body/eval_jaxpr/ppermute | solution.py:13
  1056.3 2.7 fusion.26
  1059.1 26.6 %all-reduce.3.cloned.1.call-done = bf16[1,256,512]{2,1,0:T(8,128)(2,1)} async-done(((bf16[1,256,512]{2,1,0:T(8,128)(2,1)}), bf16[1,256,512]{2,1,0:T(8,128)(2,1)}) %all-reduce.3.cloned.1.call-update) | async-done | bytes 262160 | tf_op jit(solution)/shard_map/psum | solution.py:169
  1087.5 33.4 %all-reduce.5.cloned.1.call-done = bf16[256,512]{1,0:T(8,128)(2,1)} async-done(((bf16[256,512]{1,0:T(8,128)(2,1)}), bf16[256,512]{1,0:T(8,128)(2,1)}) %all-reduce.5.cloned.1.call-update) | async-done | bytes 262160 | tf_op jit(solution)/shard_map/psum | solution.py:18
  1122.0 157.9 %psum.23 = bf16[512,16]{0,1:T(8,128)(2,1)S(1)} all-reduce(bf16[512,16]{0,1:T(8,128)(2,1)S(1)} %convolution_convert_fusion.3), channel_id=1, replica_groups=mesh['section'=2,'tp'=2,'dp'=32] {'dp'}, use_global_device_ids=true, to_apply=%region_16.17 | all-reduce | flops 8192 | bytes 32768 | tf_op jit(solution)/shard_map/psum | solution.py:177
  (120 shorter events, 54.5 us)
Async XLA Ops:
  7.2 1049.1 %copy-start = (bf16[2048,512]{1,0:T(8,128)(2,1)S(1)}, bf16[2048,512]{1,0:T(8,128)(2,1)}, u32[]{:S(2)}) copy-start(bf16[2048,512]{1,0:T(8,128)(2,1)} %param.35) | copy-start | bytes 6291460
  7.2 3.4 copy-start.10
  7.2 196.3 %all-gather.7.cloned.1.call-start = ((), (), s32[]{:S(2)}) async-start(), calls=%async_computation.1 | async-start | bytes 8650752 | tf_op jit(solution)/shard_map/all_gather | solution.py:92
  10.5 2.5 copy-start.16
  10.5 2.5 copy-start.17
  10.6 729.5 %all-gather.5.cloned.1.call-start = ((), (), s32[]{:S(2)}) async-start(), calls=%async_computation | async-start | bytes 25952256 | tf_op jit(solution)/shard_map/all_gather | solution.py:91
  13.1 3.4 copy-start.15
  13.1 4.3 copy-start.14
  13.1 1.7 copy-start.9
  16.5 2.8 copy-start.8
  740.0 4.6 copy-start.11
  740.0 4.6 copy-start.18
  744.6 18.6 %all-gather.9.cloned.1.call-start = ((), (), s32[]{:S(2)}) async-start(), calls=%async_computation.4 | async-start | bytes 6291456 | tf_op jit(solution)/shard_map/while/body/eval_jaxpr/all_gather | solution.py:122
  747.8 83.9 %all-gather.11.cloned.1.call-start = ((), (), s32[]{:S(2)}) async-start(), calls=%async_computation.5 | async-start | bytes 3145728 | tf_op jit(solution)/shard_map/while/body/eval_jaxpr/all_gather | solution.py:131
  764.4 3.4 copy-start.1
  831.7 13.0 %copy-start.3 = (bf16[1,256,512]{2,1,0:T(8,128)(2,1)S(1)}, bf16[1,256,512]{2,1,0:T(8,128)(2,1)}, u32[]{:S(2)}) copy-start(bf16[1,256,512]{2,1,0:T(8,128)(2,1)} %get-tuple-element.507) | copy-start | bytes 786436 | tf_op jit(solution)/shard_map/while
  831.7 13.0 %copy-start.6 = (bf16[256,512]{1,0:T(8,128)(2,1)S(1)}, bf16[256,512]{1,0:T(8,128)(2,1)}, u32[]{:S(2)}) copy-start(bf16[256,512]{1,0:T(8,128)(2,1)} %get-tuple-element.505) | copy-start | bytes 786436 | tf_op jit(solution)/shard_map/while
  842.2 52.7 %collective-permute-start = (bf16[512,2048]{1,0:T(8,128)(2,1)}, bf16[512,2048]{1,0:T(8,128)(2,1)}, u32[]{:S(2)}, u32[]{:S(2)}) collective-permute-start(bf16[512,2048]{1,0:T(8,128)(2,1)} %get-tuple-element.540), channel_id=1, source_target_pairs={{0,64},{1,65},{2,66},{3,67},{4,68},{5,69},{6,70},{7,71},{8,72},{9,... | collective-permute-start | bytes 6291464 | tf_op jit(solution)/shard_map/while/body/eval_jaxpr/ppermute | solution.py:13
  845.8 5.1 copy-start.4
  845.9 49.1 %collective-permute-start.1 = (bf16[256,512]{1,0:T(8,128)(2,1)S(1)}, bf16[256,512]{1,0:T(8,128)(2,1)S(1)}, u32[]{:S(2)}, u32[]{:S(2)}) collective-permute-start(bf16[256,512]{1,0:T(8,128)(2,1)S(1)} %get-tuple-element.449), channel_id=1, source_target_pairs={{0,64},{1,65},{2,66},{3,67},{4,68},{5,69},{6,70},{7,71},{8,72},{9,... | collective-permute-start | bytes 786440 | tf_op jit(solution)/shard_map/while/body/eval_jaxpr/ppermute | solution.py:13
  895.6 23.3 %all-gather.9.cloned.1.call-start = ((), (), s32[]{:S(2)}) async-start(), calls=%async_computation.4 | async-start | bytes 6291456 | tf_op jit(solution)/shard_map/while/body/eval_jaxpr/all_gather | solution.py:122
  898.8 90.2 %all-gather.11.cloned.1.call-start = ((), (), s32[]{:S(2)}) async-start(), calls=%async_computation.5 | async-start | bytes 3145728 | tf_op jit(solution)/shard_map/while/body/eval_jaxpr/all_gather | solution.py:131
  989.0 16.7 %copy-start.3 = (bf16[1,256,512]{2,1,0:T(8,128)(2,1)S(1)}, bf16[1,256,512]{2,1,0:T(8,128)(2,1)}, u32[]{:S(2)}) copy-start(bf16[1,256,512]{2,1,0:T(8,128)(2,1)} %get-tuple-element.507) | copy-start | bytes 786436 | tf_op jit(solution)/shard_map/while
  989.0 16.7 %copy-start.6 = (bf16[256,512]{1,0:T(8,128)(2,1)S(1)}, bf16[256,512]{1,0:T(8,128)(2,1)}, u32[]{:S(2)}) copy-start(bf16[256,512]{1,0:T(8,128)(2,1)} %get-tuple-element.505) | copy-start | bytes 786436 | tf_op jit(solution)/shard_map/while
  989.0 66.6 %collective-permute-start = (bf16[512,2048]{1,0:T(8,128)(2,1)}, bf16[512,2048]{1,0:T(8,128)(2,1)}, u32[]{:S(2)}, u32[]{:S(2)}) collective-permute-start(bf16[512,2048]{1,0:T(8,128)(2,1)} %get-tuple-element.540), channel_id=1, source_target_pairs={{0,64},{1,65},{2,66},{3,67},{4,68},{5,69},{6,70},{7,71},{8,72},{9,... | collective-permute-start | bytes 6291464 | tf_op jit(solution)/shard_map/while/body/eval_jaxpr/ppermute | solution.py:13
  1006.8 4.5 copy-start.4
  1006.8 48.8 %collective-permute-start.1 = (bf16[256,512]{1,0:T(8,128)(2,1)S(1)}, bf16[256,512]{1,0:T(8,128)(2,1)S(1)}, u32[]{:S(2)}, u32[]{:S(2)}) collective-permute-start(bf16[256,512]{1,0:T(8,128)(2,1)S(1)} %get-tuple-element.449), channel_id=1, source_target_pairs={{0,64},{1,65},{2,66},{3,67},{4,68},{5,69},{6,70},{7,71},{8,72},{9,... | collective-permute-start | bytes 786440 | tf_op jit(solution)/shard_map/while/body/eval_jaxpr/ppermute | solution.py:13
  1056.3 29.4 %copy-start.5 = (bf16[1,256,512]{2,1,0:T(8,128)(2,1)S(1)}, bf16[1,256,512]{2,1,0:T(8,128)(2,1)}, u32[]{:S(2)}) copy-start(bf16[1,256,512]{2,1,0:T(8,128)(2,1)} %get-tuple-element.210) | copy-start | bytes 786436
  1056.3 29.4 %all-reduce.3.cloned.1.call-start = ((), (), s32[]{:S(2)}) async-start(), calls=%async_computation.2 | async-start | bytes 524288 | tf_op jit(solution)/shard_map/psum | solution.py:169
  1056.3 64.6 %copy-start.13 = (bf16[1,256,16]{1,2,0:T(8,128)(2,1)S(1)}, bf16[1,256,16]{1,2,0:T(8,128)(2,1)}, u32[]{:S(2)}) copy-start(bf16[1,256,16]{1,2,0:T(8,128)(2,1)} %param.37) | copy-start | bytes 24580
  1056.3 224.2 %copy-start.12 = (bf16[512,16]{0,1:T(8,128)(2,1)S(1)}, bf16[512,16]{0,1:T(8,128)(2,1)}, u32[]{:S(2)}) copy-start(bf16[512,16]{0,1:T(8,128)(2,1)} %param.36) | copy-start | bytes 49156
  1059.0 61.8 %all-reduce.5.cloned.1.call-start = ((), (), s32[]{:S(2)}) async-start(), calls=%async_computation.3 | async-start | bytes 524288 | tf_op jit(solution)/shard_map/psum | solution.py:18
  (4 other events, 3.4 us)
Sparse Core Ops, SparseCore 0:
  10.7 192.7 all-gather.6
  205.1 534.8 all-gather.4
  747.9 15.2 all-gather.8
  818.6 13.0 all-gather.10
  898.9 19.9 all-gather.8
  921.4 67.5 all-gather.10
  1059.6 26.0 all-reduce.2
  1088.2 32.6 all-reduce.4
where the time goes:
time: 1290 us
  waiting for transfers between devices  973 us (75%)
  blocking collectives  158 us (12%)
  matrix products  63.7 us (5%)
  other arithmetic  29.3 us (2%)
  local copies, waits for them, and re-layouts  25.8 us (2%)
  starting transfers between devices  22.1 us (2%)
  between operations  15.5 us (1%)
    all_gather x1, waiting for transfers between devices, shards(): lax.all_gather(w_qkv, 'dp', axis=1, tiled=True)  537 us
    all_gather x1, waiting for transfers between devices, shards(): lax.all_gather(w_out, 'dp', axis=1, tiled=True)  175 us
    psum x1, blocking collectives, shards(): lax.psum(grad_local.astype(jnp.bfloat16), 'dp').astype(jnp.float32)  158 us
    ppermute x4, waiting for transfers between devices, passed_along(): return lax.ppermute(value, axis, pairs)  88.3 us
    all_gather x2, waiting for transfers between devices, tick(): all_heads = lax.all_gather(local_heads, 'tp', axis=1, tiled=True)  81 us
    psum x1, waiting for transfers between devices, broadcast(): return lax.psum(block, axis)  33.4 us
    all_gather x2, waiting for transfers between devices, tick(): full = lax.all_gather(current, 'tp', axis=1, tiled=True)  32.7 us
    psum x1, waiting for transfers between devices, shards(): lax.psum(partial_value.astype(jnp.bfloat16), 'tp').astype(jnp.float32)  26.6 us
  transfers between devices with their start and end apart: 12, of which 10 were waited for; matrix products, arithmetic and copies ran while one was open for 2% of the time, Pallas kernels for 0%

commit v1 on v0

--- a/solution.py
+++ b/solution.py
@@ -119,7 +119,9 @@
         slot = jnp.clip(index, 0, micro - 1)
         current = jnp.where(section == 0, lax.dynamic_index_in_dim(embedded, slot, 0, False), inbox)
         allowed = lax.dynamic_index_in_dim(masks, slot, 0, False)
-        full = lax.all_gather(current, "tp", axis=1, tiled=True)
+        full = jnp.concatenate(
+            lax.all_to_all(jnp.stack([current] * lax.axis_size("tp")), "tp", 0, 0), axis=1
+        )
 
         def attend_live(unused):
             return attend(rms_normed(full, gain), qkv_layer, allowed)

time: 1290 us -> 1340 us (1.039)
  other arithmetic: 29.3 us -> 46 us
  local copies, waits for them, and re-layouts: 25.8 us -> 42.2 us
    all_gather x2 -> x0, waiting for transfers between devices: 32.7 us -> none  [tick(): full = lax.all_gather(current, 'tp', axis=1, tiled=True)]
    all_gather x2, waiting for transfers between devices: 81 us -> 111 us  [tick(): all_heads = lax.all_gather(local_heads, 'tp', axis=1, tiled=True)]
    cond x4 -> x1, local copies, waits for them, and re-layouts: 0.87 us -> 14.7 us
where the time goes in v1:
time: 1340 us
  waiting for transfers between devices  976 us (73%)
  blocking collectives  158 us (12%)
  matrix products  66.7 us (5%)
  other arithmetic  46 us (3%)
  local copies, waits for them, and re-layouts  42.2 us (3%)
  starting transfers between devices  33.3 us (2%)
  between operations  15.5 us (1%)
    all_gather x1, waiting for transfers between devices, shards(): lax.all_gather(w_qkv, 'dp', axis=1, tiled=True)  537 us
    all_gather x1, waiting for transfers between devices, shards(): lax.all_gather(w_out, 'dp', axis=1, tiled=True)  174 us
    psum x1, blocking collectives, shards(): lax.psum(grad_local.astype(jnp.bfloat16), 'dp').astype(jnp.float32)  158 us
    all_gather x2, waiting for transfers between devices, tick(): all_heads = lax.all_gather(local_heads, 'tp', axis=1, tiled=True)  111 us
    ppermute x4, waiting for transfers between devices, passed_along(): return lax.ppermute(value, axis, pairs)  88.3 us
    psum x1, waiting for transfers between devices, broadcast(): return lax.psum(block, axis)  33.2 us
  transfers between devices with their start and end apart: 12, of which 10 were waited for; matrix products, arithmetic and copies ran while one was open for 2% of the time, Pallas kernels for 0%

profile of v1, /device:TPU:0, one launch (start us, length us, event | category | flops | bytes accessed | tf_op | source)
XLA Modules:
  0.0 1339.3 jit_solution(10049314391580131133)
XLA Ops:
  7.3 3.4 copy.68
  13.2 3.4 conditional.3
  19.5 3.3 select_select_fusion
  22.8 6.5 select_n.85
  29.3 174.3 %all-gather.6.cloned.1.call-done = bf16[1,2048,2048]{2,1,0:T(8,128)(2,1)} async-done(((bf16[1,64,2048]{2,1,0:T(8,128)(2,1)}), bf16[1,2048,2048]{2,1,0:T(8,128)(2,1)}) %all-gather.6.cloned.1.call-update) | async-done | bytes 8388624 | tf_op jit(solution)/shard_map/all_gather | solution.py:92
  203.6 536.5 %all-gather.4.cloned.1.call-done = bf16[1,4096,8,3,128]{4,1,3,2,0:T(8,128)(2,1)} async-done(((bf16[1,128,8,3,128]{4,1,3,2,0:T(8,128)(2,1)}), bf16[1,4096,8,3,128]{4,1,3,2,0:T(8,128)(2,1)}) %all-gather.4.cloned.1.call-update) | async-done | bytes 25165840 | tf_op jit(solution)/shard_map/all_gather | solution.py:91
  744.7 362.3 %while.30 = (s32[]{:T(128)}, bf16[512,2048]{1,0:T(8,128)(2,1)}, bf16[256,512]{1,0:T(8,128)(2,1)}, bf16[1,512,2048]{2,1,0:T(8,128)(2,1)}, bf16[1,256,512]{2,1,0:T...) while((s32[]{:T(128)}, bf16[512,2048]{1,0:T(8,128)(2,1)}, ...), condition=%wide.region_13.14_spmd.clone, body=%wide.region_3.13_spmd.clone.sunk | while | flops 17341415424 | bytes 163882848 | solution.py:164
  747.8 2.4 pad_maximum_fusion.2
  750.3 5.6 all-to-all-start
  757.1 3.2 all-to-all-done
  761.5 84.1 %conditional.8 = (bf16[512,1024]{1,0:T(8,128)(2,1)S(1)}) conditional(s32[]{:T(128)} %convert_element_type.131, () %tuple.86, (bf16[512,2,2048]{2,0,1:T(8,128)(2,1)}, f32[1,4096]{1,0:T(1,128)S(1)}, bf16[4096,8,3,128]{3,0,2,1:T(8,128)(2,1)}, s32[512]{0:T(512)S(1)}, s32[1,512,512]{1,2,0:T(8,128)S(1)}, /*index=5*/s32[512]{0:T(512)S(1)}, ...), branch_computations={%region_4.4_spmd, %region_5.10_spmd} | conditional | flops 13038844928 | bytes 78685384 | solution.py:132
  761.5 9.8 copy_convert_fusion
  771.3 14.7 %copy.25 = f32[64,8,2,2048]{3,1,2,0:T(8,128)} copy(f32[64,8,2,2048]{3,2,1,0:T(2,128)} %bitcast.122) | data formatting | bytes 16777216 | tf_op jit(solution)/shard_map/while/body/eval_jaxpr/cond
  786.0 7.6 multiply_reduce_fusion
  793.7 21.5 %convert_bitcast_fusion = bf16[8,3,512,128]{3,2,1,0:T(8,128)(2,1)} fusion(bf16[4096,8,3,128]{3,0,2,1:T(8,128)(2,1)} %get-tuple-element.179, f32[512,4096]{1,0:T(8,128)} %bitcast.124, f32[4096]{0:T(1024)S(1)} %bitcast.129, f32[512]{0:T(512)S(1)} %add_rsqrt_fusion), kind=kOutput, calls=%fused_computation.27 | convolution fusion | flops 12892766208 | bytes 36718592 | tf_op jit(solution)/shard_map/while/body/eval_jaxpr/cond/branch_1_fun/rd,dhtk->htrk/dot_general | solution.py:53
  816.8 27.5 %while.29 = (s32[]{:T(128)}, bf16[8,512,128]{2,1,0:T(8,128)(2,1)}, bf16[8,3,512,128]{3,2,1,0:T(8,128)(2,1)}, pred[512,512]{0,1:T(32,128)(4,1)S(1)}, s32[]{:T(128)}, /*index=5*/s32[]{:T(128)}, s32[]{}, s32[]{}) while((s32[]{:T(128)}, bf16[8,512,128]{2,1,0:T(8,128)(2,1)}, bf16[8,3,512,128]{3,2,1,0:T(8,128)(2,1)}, ...), condition=%wide.region_10.9_spmd, body=%wide.region_7.8_spmd.sunk | while | flops 136379392 | bytes 3944565 | solution.py:65
  846.6 10.2 all-gather.8.cloned.1.call-done
  856.8 10.4 conditional.9
  856.8 10.4 add_convert_fusion
  867.2 2.6 collective-permute-start
  872.2 3.8 fusion.55
  876.0 44.0 %collective-permute-done.1 = bf16[256,512]{1,0:T(8,128)(2,1)S(1)} collective-permute-done((bf16[256,512]{1,0:T(8,128)(2,1)S(1)}, bf16[256,512]{1,0:T(8,128)(2,1)S(1)}, u32[]{:S(2)}, u32[]{:S(2)}) %collective-permute-start.1) | collective-permute-done | bytes 262176 | tf_op jit(solution)/shard_map/while/body/eval_jaxpr/ppermute | solution.py:13
  926.2 5.6 all-to-all-start
  933.1 3.2 all-to-all-done
  938.6 101.0 %all-gather.8.cloned.1.call-done = bf16[512,2048]{1,0:T(8,128)(2,1)} async-done(((bf16[512,1024]{1,0:T(8,128)(2,1)}), bf16[512,2048]{1,0:T(8,128)(2,1)}) %all-gather.8.cloned.1.call-update) | async-done | bytes 2097168 | tf_op jit(solution)/shard_map/while/body/eval_jaxpr/all_gather | solution.py:133
  1039.7 16.7 %collective-permute-start = (bf16[512,2048]{1,0:T(8,128)(2,1)}, bf16[512,2048]{1,0:T(8,128)(2,1)}, u32[]{:S(2)}, u32[]{:S(2)}) collective-permute-start(bf16[512,2048]{1,0:T(8,128)(2,1)} %get-tuple-element.545), channel_id=1, source_target_pairs={{0,64},{1,65},{2,66},{3,67},{4,68},{5,69},{6,70},{7,71},{8,72},{9,... | collective-permute-start | bytes 6291464 | tf_op jit(solution)/shard_map/while/body/eval_jaxpr/ppermute | solution.py:13
  1058.8 3.1 fusion.55
  1061.9 44.3 %collective-permute-done.1 = bf16[256,512]{1,0:T(8,128)(2,1)S(1)} collective-permute-done((bf16[256,512]{1,0:T(8,128)(2,1)S(1)}, bf16[256,512]{1,0:T(8,128)(2,1)S(1)}, u32[]{:S(2)}, u32[]{:S(2)}) %collective-permute-start.1) | collective-permute-done | bytes 262176 | tf_op jit(solution)/shard_map/while/body/eval_jaxpr/ppermute | solution.py:13
  1107.0 2.7 fusion.23
  1109.8 26.2 %all-reduce.3.cloned.1.call-done = bf16[1,256,512]{2,1,0:T(8,128)(2,1)} async-done(((bf16[1,256,512]{2,1,0:T(8,128)(2,1)}), bf16[1,256,512]{2,1,0:T(8,128)(2,1)}) %all-reduce.3.cloned.1.call-update) | async-done | bytes 262160 | tf_op jit(solution)/shard_map/psum | solution.py:171
  1137.9 33.2 %all-reduce.5.cloned.1.call-done = bf16[256,512]{1,0:T(8,128)(2,1)} async-done(((bf16[256,512]{1,0:T(8,128)(2,1)}), bf16[256,512]{1,0:T(8,128)(2,1)}) %all-reduce.5.cloned.1.call-update) | async-done | bytes 262160 | tf_op jit(solution)/shard_map/psum | solution.py:18
  1172.2 157.9 %psum.23 = bf16[512,16]{0,1:T(8,128)(2,1)S(1)} all-reduce(bf16[512,16]{0,1:T(8,128)(2,1)S(1)} %convolution_convert_fusion.3), channel_id=1, replica_groups=mesh['section'=2,'tp'=2,'dp'=32] {'dp'}, use_global_device_ids=true, to_apply=%region_16.17 | all-reduce | flops 8192 | bytes 32768 | tf_op jit(solution)/shard_map/psum | solution.py:179
  (122 shorter events, 68.7 us)
Async XLA Ops:
  7.2 1099.8 %copy-start = (bf16[2048,512]{1,0:T(8,128)(2,1)S(1)}, bf16[2048,512]{1,0:T(8,128)(2,1)}, u32[]{:S(2)}) copy-start(bf16[2048,512]{1,0:T(8,128)(2,1)} %param.35) | copy-start | bytes 6291460
  7.2 3.5 copy-start.9
  7.2 5.9 copy-start.16
  7.2 5.9 copy-start.15
  7.2 196.4 %all-gather.6.cloned.1.call-start = ((), (), s32[]{:S(2)}) async-start(), calls=%async_computation.2 | async-start | bytes 8650752 | tf_op jit(solution)/shard_map/all_gather | solution.py:92
  10.6 729.5 %all-gather.4.cloned.1.call-start = ((), (), s32[]{:S(2)}) async-start(), calls=%async_computation.1 | async-start | bytes 25952256 | tf_op jit(solution)/shard_map/all_gather | solution.py:91
  13.2 3.5 copy-start.14
  13.2 4.3 copy-start.13
  16.6 2.9 copy-start.8
  22.8 721.9 %copy-start.10 = (s32[1,512]{1,0:T(1,128)S(1)}, s32[1,512]{1,0:T(1,128)}, u32[]{:S(2)}) copy-start(s32[1,512]{1,0:T(1,128)} %param.27) | copy-start | bytes 6148
  22.8 721.9 %copy-start.17 = (f32[1,4096]{1,0:T(1,128)S(1)}, f32[1,4096]{1,0:T(1,128)}, u32[]{:S(2)}) copy-start(f32[1,4096]{1,0:T(1,128)} %param.30) | copy-start | bytes 49156
  746.5 1.3 copy-start.1
  750.3 10.0 all-to-all-start
  755.8 101.0 %all-gather.8.cloned.1.call-start = ((), (), s32[]{:S(2)}) async-start(), calls=%async_computation.5 | async-start | bytes 3145728 | tf_op jit(solution)/shard_map/while/body/eval_jaxpr/all_gather | solution.py:133
  856.8 13.0 copy-start.3
  856.8 13.0 copy-start.6
  867.2 52.7 %collective-permute-start = (bf16[512,2048]{1,0:T(8,128)(2,1)}, bf16[512,2048]{1,0:T(8,128)(2,1)}, u32[]{:S(2)}, u32[]{:S(2)}) collective-permute-start(bf16[512,2048]{1,0:T(8,128)(2,1)} %get-tuple-element.545), channel_id=1, source_target_pairs={{0,64},{1,65},{2,66},{3,67},{4,68},{5,69},{6,70},{7,71},{8,72},{9,... | collective-permute-start | bytes 6291464 | tf_op jit(solution)/shard_map/while/body/eval_jaxpr/ppermute | solution.py:13
  870.9 5.1 copy-start.4
  870.9 49.0 %collective-permute-start.1 = (bf16[256,512]{1,0:T(8,128)(2,1)S(1)}, bf16[256,512]{1,0:T(8,128)(2,1)S(1)}, u32[]{:S(2)}, u32[]{:S(2)}) collective-permute-start(bf16[256,512]{1,0:T(8,128)(2,1)S(1)} %get-tuple-element.454), channel_id=1, source_target_pairs={{0,64},{1,65},{2,66},{3,67},{4,68},{5,69},{6,70},{7,71},{8,72},{9,... | collective-permute-start | bytes 786440 | tf_op jit(solution)/shard_map/while/body/eval_jaxpr/ppermute | solution.py:13
  922.5 1.3 copy-start.1
  926.2 10.0 all-to-all-start
  931.8 107.8 %all-gather.8.cloned.1.call-start = ((), (), s32[]{:S(2)}) async-start(), calls=%async_computation.5 | async-start | bytes 3145728 | tf_op jit(solution)/shard_map/while/body/eval_jaxpr/all_gather | solution.py:133
  1039.6 16.7 %copy-start.3 = (bf16[1,256,512]{2,1,0:T(8,128)(2,1)S(1)}, bf16[1,256,512]{2,1,0:T(8,128)(2,1)}, u32[]{:S(2)}) copy-start(bf16[1,256,512]{2,1,0:T(8,128)(2,1)} %get-tuple-element.512) | copy-start | bytes 786436 | tf_op jit(solution)/shard_map/while
  1039.6 16.7 %copy-start.6 = (bf16[256,512]{1,0:T(8,128)(2,1)S(1)}, bf16[256,512]{1,0:T(8,128)(2,1)}, u32[]{:S(2)}) copy-start(bf16[256,512]{1,0:T(8,128)(2,1)} %get-tuple-element.510) | copy-start | bytes 786436 | tf_op jit(solution)/shard_map/while
  1039.7 66.6 %collective-permute-start = (bf16[512,2048]{1,0:T(8,128)(2,1)}, bf16[512,2048]{1,0:T(8,128)(2,1)}, u32[]{:S(2)}, u32[]{:S(2)}) collective-permute-start(bf16[512,2048]{1,0:T(8,128)(2,1)} %get-tuple-element.545), channel_id=1, source_target_pairs={{0,64},{1,65},{2,66},{3,67},{4,68},{5,69},{6,70},{7,71},{8,72},{9,... | collective-permute-start | bytes 6291464 | tf_op jit(solution)/shard_map/while/body/eval_jaxpr/ppermute | solution.py:13
  1057.5 4.5 copy-start.4
  1057.5 48.8 %collective-permute-start.1 = (bf16[256,512]{1,0:T(8,128)(2,1)S(1)}, bf16[256,512]{1,0:T(8,128)(2,1)S(1)}, u32[]{:S(2)}, u32[]{:S(2)}) collective-permute-start(bf16[256,512]{1,0:T(8,128)(2,1)S(1)} %get-tuple-element.454), channel_id=1, source_target_pairs={{0,64},{1,65},{2,66},{3,67},{4,68},{5,69},{6,70},{7,71},{8,72},{9,... | collective-permute-start | bytes 786440 | tf_op jit(solution)/shard_map/while/body/eval_jaxpr/ppermute | solution.py:13
  1107.0 29.1 %copy-start.5 = (bf16[1,256,512]{2,1,0:T(8,128)(2,1)S(1)}, bf16[1,256,512]{2,1,0:T(8,128)(2,1)}, u32[]{:S(2)}) copy-start(bf16[1,256,512]{2,1,0:T(8,128)(2,1)} %get-tuple-element.211) | copy-start | bytes 786436
  1107.0 64.2 %copy-start.12 = (bf16[1,256,16]{1,2,0:T(8,128)(2,1)S(1)}, bf16[1,256,16]{1,2,0:T(8,128)(2,1)}, u32[]{:S(2)}) copy-start(bf16[1,256,16]{1,2,0:T(8,128)(2,1)} %param.37) | copy-start | bytes 24580
  1107.0 223.8 %copy-start.11 = (bf16[512,16]{0,1:T(8,128)(2,1)S(1)}, bf16[512,16]{0,1:T(8,128)(2,1)}, u32[]{:S(2)}) copy-start(bf16[512,16]{0,1:T(8,128)(2,1)} %param.36) | copy-start | bytes 49156
  1107.0 29.1 %all-reduce.3.cloned.1.call-start = ((), (), s32[]{:S(2)}) async-start(), calls=%async_computation.3 | async-start | bytes 524288 | tf_op jit(solution)/shard_map/psum | solution.py:171
  1109.7 61.4 %all-reduce.5.cloned.1.call-start = ((), (), s32[]{:S(2)}) async-start(), calls=%async_computation.4 | async-start | bytes 524288 | tf_op jit(solution)/shard_map/psum | solution.py:18
  (4 other events, 3.4 us)
Sparse Core Ops, SparseCore 0:
  10.8 192.7 all-gather.5
  205.2 534.8 all-gather.3
  846.8 9.9 all-gather.7
  938.7 100.8 all-gather.7
  1109.9 26.0 all-reduce.2
  1138.5 32.6 all-reduce.4
